TPU v7x, 32 devices: a whole 2x2x4 slice. The times are simulated.
32 devices in a mesh: space: 8 (over y, x, core), tm: 4 (over z).
Axes of the slice: x: 2, y: 2, z: 4, core: 2. Of those that a mesh axis runs over, the one named last changes fastest.
Arguments:
- residual_in: float32 [32768, 2048], P('space', 'tm'), may hold values from -6 to 6
- factor_panel: float32 [32768, 1024], P('space'), may hold values from -0.1875 to 0.1875
- diag_inverse: float32 [4, 256, 256], replicated, may hold values from -2 to 2, as said below
- time_inverse: float32 [2048, 2048], P('space'), may hold values from -2 to 2, as said below
Outputs:
- whitened: float32 [32768, 2048], P(('space', 'tm'))
Inputs may be any that keep to these rules, and one draw needn't show every extreme that they name: `diag_inverse`: lower triangular, with diagonal entries between 0.5 and 2. `time_inverse`: lower triangular, with diagonal entries between 0.5 and 2.
All inputs are finite; a program needn't handle non-finite values.
Results may differ from a plain program's by a relative error of at most 0.0001.
Values sent between devices are 32-bit elements; how exact they have to be, the bound alone decides.
No kernel may reach another device: no remote copies, remote signals or barrier semaphores. Data moves between devices by JAX's collectives and lax.ppermute only.
A program may use at most 128 MiB of HBM per device.

v0:
```python
import jax
import jax.numpy as jnp
from jax import lax
from jax.sharding import PartitionSpec as P


def broadcast(block, axis, owner):
    block = jnp.where(lax.axis_index(axis) == owner, block, jnp.zeros_like(block))
    return lax.psum(block, axis)


def product(left, right):
    return jnp.dot(left, right, precision=lax.Precision.HIGHEST, preferred_element_type=jnp.float32)


def product_by_rows(left, right):
    return lax.dot_general(
        left,
        right,
        (((1,), (1,)), ((), ())),
        precision=lax.Precision.HIGHEST,
        preferred_element_type=jnp.float32,
    )


def share(candidate, current):
    return broadcast(candidate, "space", current)


def shards(residual_in, factor_panel, diag_inverse, time_inverse):
    width = diag_inverse.shape[1]
    steps_total = diag_inverse.shape[0]
    position = lax.axis_index("space")
    head_rows = residual_in[:width]
    tail_rows = residual_in[width:]
    candidate = product(diag_inverse[0], head_rows)
    for current in range(steps_total):
        solved = share(candidate, current)
        columns = factor_panel[:, current * width : (current + 1) * width]
        head_rows = jnp.where(
            position > current,
            head_rows - product(columns[:width], solved),
            jnp.where(position == current, solved, head_rows),
        )
        if current + 1 < steps_total:
            candidate = product(diag_inverse[current + 1], head_rows)
        tail_rows = tail_rows - product(columns[width:], solved)
    values = jnp.concatenate([head_rows, tail_rows], 0)
    turned = lax.all_to_all(values, "tm", split_axis=0, concat_axis=1, tiled=True)
    return product_by_rows(turned, lax.all_gather(time_inverse, "space", axis=0, tiled=True))


def solution(mesh):
    in_specs = (P("space", "tm"), P("space", None), P(), P("space", None))
    out_specs = P(("space", "tm"), None)
    return jax.shard_map(shards, mesh=mesh, in_specs=in_specs, out_specs=out_specs, check_vma=False)
```

profile of v0, /device:TPU:0, one launch (start us, length us, event | category | flops | bytes accessed | tf_op | source)
XLA Modules:
  0.0 592.7 jit_solution(16608482617738462351)
XLA Ops:
  6.5 2.5 convolution_select_fusion.3
  9.1 58.8 %all-reduce.5.cloned.1.call-done = f32[256,512]{1,0:T(8,128)} async-done(((f32[256,512]{1,0:T(8,128)}), f32[256,512]{1,0:T(8,128)}) %all-reduce.5.cloned.1.call-update) | async-done | bytes 524304 | tf_op jit(solution)/shard_map/psum | solution.py:9
  68.0 2.1 fusion.11
  70.1 2.4 fusion.9
  72.6 54.2 %all-reduce.7.cloned.1.call-done = f32[256,512]{1,0:T(8,128)} async-done(((f32[256,512]{1,0:T(8,128)}), f32[256,512]{1,0:T(8,128)}) %all-reduce.7.cloned.1.call-update) | async-done | bytes 524304 | tf_op jit(solution)/shard_map/psum | solution.py:9
  126.8 2.0 fusion.13
  128.7 2.4 fusion.8
  131.2 54.2 %all-reduce.9.cloned.1.call-done = f32[256,512]{1,0:T(8,128)} async-done(((f32[256,512]{1,0:T(8,128)}), f32[256,512]{1,0:T(8,128)}) %all-reduce.9.cloned.1.call-update) | async-done | bytes 524304 | tf_op jit(solution)/shard_map/psum | solution.py:9
  185.4 2.0 fusion.15
  187.4 2.4 fusion.7
  189.8 0.3 all-gather.2.cloned.1.call-start
  190.2 0.2 all-gather.2.cloned.1.call-update
  190.4 7.4 %slice.63 = f32[3840,512]{1,0:T(8,128)} slice(f32[4096,512]{1,0:T(8,128)} %param.4), slice={[256:4096], [0:512]} | slice | bytes 15728640 | tf_op jit(solution)/shard_map/slice | solution.py:35
  197.8 9.2 %copy.19 = f32[3840,512]{0,1:T(8,128)} copy(f32[3840,512]{1,0:T(8,128)} %slice.63) | data formatting | bytes 15728640
  207.0 17.2 %fusion.5 = f32[512,3840]{1,0:T(8,128)} fusion(f32[256,512]{1,0:T(8,128)S(1)} %copy-done, f32[4096,1024]{1,0:T(8,128)} %param.5), kind=kOutput, calls=%fused_computation.11 | convolution fusion | flops 6039797760 | bytes 12320768 | tf_op jit(solution)/shard_map/dot_general | solution.py:13
  224.1 17.5 %fusion.3 = f32[512,3840]{1,0:T(8,128)} fusion(f32[256,512]{1,0:T(8,128)S(1)} %copy-done.1, f32[4096,1024]{1,0:T(8,128)} %param.5), kind=kOutput, calls=%fused_computation.9 | convolution fusion | flops 6039797760 | bytes 12320768 | tf_op jit(solution)/shard_map/dot_general | solution.py:13
  241.7 17.2 %fusion.1 = f32[512,3840]{1,0:T(8,128)} fusion(f32[256,512]{1,0:T(8,128)S(1)} %copy-done.2, f32[4096,1024]{1,0:T(8,128)} %param.5), kind=kOutput, calls=%fused_computation.7 | convolution fusion | flops 6039797760 | bytes 12320768 | tf_op jit(solution)/shard_map/dot_general | solution.py:13
  258.9 2.0 fusion.17
  260.9 1.0 copy.14
  261.9 23.3 %bitcast_subtract_fusion = f32[3840,512]{0,1:T(8,128)S(1)} fusion(f32[512,3840]{1,0:T(8,128)} %fusion.1, f32[512,3840]{1,0:T(8,128)} %fusion.3, f32[3840,512]{0,1:T(8,128)} %copy.19, f32[512,3840]{1,0:T(8,128)} %fusion.5, f32[256,512]{1,0:T(8,128)} %all-reduce.11.cloned.1.call-done, f32[4096,1024]{1,0:T(8,128)} %param.5), kind=kOutput, calls=%fused_computation.2 | convolution fusion | flops 6047662080 | bytes 43778048 | tf_op jit(solution)/shard_map/dot_general | solution.py:13
  285.2 2.2 pad_maximum_fusion
  287.4 1.7 copy.22
  289.1 186.6 %all_to_all.19 = f32[4,1024,512]{1,2,0:T(8,128)} all-to-all(f32[4,1024,512]{1,2,0:T(8,128)S(1)} %bitcast.77), channel_id=1, replica_groups=mesh['space'=8,'tm'=4] {'tm'}, dimensions={0} | all-to-all | bytes 16777216 | tf_op jit(solution)/shard_map/all_to_all | solution.py:49
  475.7 110.2 %fusion.31 = f32[1024,2048]{1,0:T(8,128)} fusion(f32[1024,2048]{0,1:T(8,128)} %bitcast.78, f32[2048,2048]{1,0:T(8,128)} %all-gather.2.cloned.1.call-done), kind=kOutput, calls=%fused_computation.45 | convolution fusion | flops 51539607552 | bytes 33554432 | tf_op jit(solution)/shard_map/dot_general | solution.py:17
  (16 shorter events, 0.2 us)
Async XLA Ops:
  6.5 61.4 %all-reduce.5.cloned.1.call-start = ((), (), s32[]{:S(2)}) async-start(), calls=%async_computation.1 | async-start | bytes 1048576 | tf_op jit(solution)/shard_map/psum | solution.py:9
  9.1 117.7 %all-reduce.7.cloned.1.call-start = ((), (), s32[]{:S(2)}) async-start(), calls=%async_computation.2 | async-start | bytes 1048576 | tf_op jit(solution)/shard_map/psum | solution.py:9
  72.5 112.9 %all-reduce.9.cloned.1.call-start = ((), (), s32[]{:S(2)}) async-start(), calls=%async_computation.3 | async-start | bytes 1048576 | tf_op jit(solution)/shard_map/psum | solution.py:9
  131.2 127.8 %all-reduce.11.cloned.1.call-start = ((), (), s32[]{:S(2)}) async-start(), calls=%async_computation.4 | async-start | bytes 1048576 | tf_op jit(solution)/shard_map/psum | solution.py:9
  189.8 285.9 %all-gather.2.cloned.1.call-start = ((), (), s32[]{:S(2)}) async-start(), calls=%async_computation.5 | async-start | bytes 18874368 | tf_op jit(solution)/shard_map/all_gather | solution.py:50
  197.8 9.2 %copy-start = (f32[256,512]{1,0:T(8,128)S(1)}, f32[256,512]{1,0:T(8,128)}, u32[]{:S(2)}) copy-start(f32[256,512]{1,0:T(8,128)} %all-reduce.5.cloned.1.call-done) | copy-start | bytes 1572868
  207.0 17.2 %copy-start.1 = (f32[256,512]{1,0:T(8,128)S(1)}, f32[256,512]{1,0:T(8,128)}, u32[]{:S(2)}) copy-start(f32[256,512]{1,0:T(8,128)} %all-reduce.7.cloned.1.call-done) | copy-start | bytes 1572868
  224.1 17.6 %copy-start.2 = (f32[256,512]{1,0:T(8,128)S(1)}, f32[256,512]{1,0:T(8,128)}, u32[]{:S(2)}) copy-start(f32[256,512]{1,0:T(8,128)} %all-reduce.9.cloned.1.call-done) | copy-start | bytes 1572868
Sparse Core Ops, SparseCore 0:
  10.4 57.4 all-reduce.4
  72.6 54.1 all-reduce.6
  131.3 54.0 all-reduce.8
  189.9 54.0 all-reduce.10
  245.8 89.0 all-gather.1
where the time goes:
time: 597 us; the launch traced here: 593 us
  matrix products  203 us (34%)
  blocking collectives  187 us (31%)
  waiting for transfers between devices  168 us (28%)
  local copies, waits for them, and re-layouts  19.2 us (3%)
  between operations  13.5 us (2%)
    all_to_all x1, blocking collectives, shards(): lax.all_to_all(values, 'tm', split_axis=0, concat_axis=1, tiled=True)  187 us
    psum x4, waiting for transfers between devices, broadcast(): return lax.psum(block, axis)  167 us
    dot_general x1, matrix products, product_by_rows(): lax.dot_general(left, right, (((1,), (1,)), ((), ())), precision=lax.Prec...  110 us
    dot_general x12, matrix products, product(): jnp.dot(left, right, precision=lax.Precision.HIGHEST, preferred_element_t...  93 us
  transfers between devices with their start and end apart: 5, of which 3 were waited for; matrix products, arithmetic and copies ran while one was open for 17% of the time, Pallas kernels for 0%

commit v1 on v0

--- a/solution.py
+++ b/solution.py
@@ -4,9 +4,14 @@
 from jax.sharding import PartitionSpec as P
 
 
+def form_tasks(matrix, chip_axis):
+    z = jnp.sum(lax.all_gather(matrix, chip_axis), axis=0)
+    return z
+
+
 def broadcast(block, axis, owner):
     block = jnp.where(lax.axis_index(axis) == owner, block, jnp.zeros_like(block))
-    return lax.psum(block, axis)
+    return form_tasks(block, chip_axis=axis)
 
 
 def product(left, right):

time: 597 us -> 555 us (0.930)
  blocking collectives: 187 us -> 0 us
  waiting for transfers between devices: 168 us -> 299 us
  matrix products: 203 us -> 186 us
  local copies, waits for them, and re-layouts: 19.2 us -> 34.9 us
  other arithmetic: 2.21 us -> 8.55 us
    all_to_all x1 -> x0, blocking collectives: 187 us -> none  [shards(): lax.all_to_all(values, 'tm', split_axis=0, concat_axis=1, tiled=True)]
    psum x4 -> x0, waiting for transfers between devices: 167 us -> none  [broadcast(): return lax.psum(block, axis)]
    all_to_all x0 -> x1, waiting for transfers between devices: none -> 151 us  [shards(): lax.all_to_all(values, 'tm', split_axis=0, concat_axis=1, tiled=True)]
    all_gather x0 -> x4, waiting for transfers between devices: none -> 114 us  [form_tasks(): z = jnp.sum(lax.all_gather(matrix, chip_axis), axis=0)]
    all_gather x1, waiting for transfers between devices: 0.01 us -> 32.9 us  [shards(): lax.all_gather(time_inverse, 'space', axis=0, tiled=True)]
    dot_general x12, matrix products: 93 us -> 76.1 us  [product(): jnp.dot(left, right, precision=lax.Precision.HIGHEST, preferred_element_t...]
    unnamed x7 -> x6, local copies, waits for them, and re-layouts: 9.22 us -> 21.7 us
    reduce_sum x0 -> x4, other arithmetic: none -> 6.5 us  [form_tasks(): z = jnp.sum(lax.all_gather(matrix, chip_axis), axis=0)]
  transfers between devices with their start and end apart: 5 -> 6, of which waited for: 3 -> 5; matrix products, arithmetic and copies ran while one was open for 17% -> 16% of each run, Pallas kernels for 0% -> 0%
where the time goes in v1:
time: 555 us; the launch traced here: 548 us
  waiting for transfers between devices  299 us (54%)
  matrix products  186 us (34%)
  local copies, waits for them, and re-layouts  34.9 us (6%)
  between operations  13.5 us (2%)
  other arithmetic  8.55 us (2%)
  starting transfers between devices  6 us (1%)
    all_to_all x1, waiting for transfers between devices, shards(): lax.all_to_all(values, 'tm', split_axis=0, concat_axis=1, tiled=True)  151 us
    all_gather x4, waiting for transfers between devices, form_tasks(): z = jnp.sum(lax.all_gather(matrix, chip_axis), axis=0)  114 us
    dot_general x1, matrix products, product_by_rows(): lax.dot_general(left, right, (((1,), (1,)), ((), ())), precision=lax.Prec...  110 us
    dot_general x12, matrix products, product(): jnp.dot(left, right, precision=lax.Precision.HIGHEST, preferred_element_t...  76.1 us
    all_gather x1, waiting for transfers between devices, shards(): lax.all_gather(time_inverse, 'space', axis=0, tiled=True)  32.9 us
    unnamed x6, local copies, waits for them, and re-layouts  21.7 us
  transfers between devices with their start and end apart: 6, of which 5 were waited for; matrix products, arithmetic and copies ran while one was open for 16% of the time, Pallas kernels for 0%

profile of v1, /device:TPU:0, one launch (start us, length us, event | category | flops | bytes accessed | tf_op | source)
XLA Modules:
  0.0 548.1 jit_solution(1220955469861362677)
XLA Ops:
  6.5 2.5 convolution_select_fusion.3
  9.1 39.4 %all-gather.12.cloned.1.call-done = f32[2048,512]{1,0:T(8,128)} async-done(((f32[256,512]{1,0:T(8,128)}), f32[2048,512]{1,0:T(8,128)}) %all-gather.12.cloned.1.call-update) | async-done | bytes 4194320 | tf_op jit(solution)/shard_map/all_gather | solution.py:8
  48.6 2.7 reduce_sum.36
  51.3 1.8 fusion.11
  53.1 2.7 fusion.9
  55.9 37.4 %all-gather.14.cloned.1.call-done = f32[2048,512]{0,1:T(8,128)} async-done(((f32[256,512]{0,1:T(8,128)}), f32[2048,512]{0,1:T(8,128)}) %all-gather.14.cloned.1.call-update) | async-done | bytes 4194320 | tf_op jit(solution)/shard_map/all_gather | solution.py:8
  93.3 4.1 copy.18
  100.6 2.7 fusion.8
  103.6 37.3 %all-gather.16.cloned.1.call-done = f32[2048,512]{0,1:T(8,128)} async-done(((f32[256,512]{0,1:T(8,128)}), f32[2048,512]{0,1:T(8,128)}) %all-gather.16.cloned.1.call-update) | async-done | bytes 4194320 | tf_op jit(solution)/shard_map/all_gather | solution.py:8
  140.9 4.1 copy.19
  148.1 2.7 fusion.7
  151.5 7.4 %slice.63 = f32[3840,512]{1,0:T(8,128)} slice(f32[4096,512]{1,0:T(8,128)} %param.4), slice={[256:4096], [0:512]} | slice | bytes 15728640 | tf_op jit(solution)/shard_map/slice | solution.py:40
  158.9 9.3 %copy.16 = f32[3840,512]{0,1:T(8,128)} copy(f32[3840,512]{1,0:T(8,128)} %slice.63) | data formatting | bytes 15728640
  168.1 17.0 %fusion.5 = f32[512,3840]{1,0:T(8,128)} fusion(f32[256,512]{1,0:T(8,128)S(1)} %reduce_sum.36, f32[4096,1024]{1,0:T(8,128)} %param.5), kind=kOutput, calls=%fused_computation.14 | convolution fusion | flops 6039797760 | bytes 12320768 | tf_op jit(solution)/shard_map/dot_general | solution.py:18
  185.2 11.0 %fusion.3 = f32[512,3840]{1,0:T(8,128)} fusion(f32[256,512]{0,1:T(8,128)S(1)} %bitcast_reduce_fusion.2, f32[4096,1024]{1,0:T(8,128)} %param.5), kind=kOutput, calls=%fused_computation.12 | convolution fusion | flops 6039797760 | bytes 12320768 | tf_op jit(solution)/shard_map/dot_general | solution.py:18
  196.2 12.1 %fusion.1 = f32[512,3840]{1,0:T(8,128)} fusion(f32[256,512]{0,1:T(8,128)S(1)} %bitcast_reduce_fusion.1, f32[4096,1024]{1,0:T(8,128)} %param.5), kind=kOutput, calls=%fused_computation.10 | convolution fusion | flops 6039797760 | bytes 12320768 | tf_op jit(solution)/shard_map/dot_general | solution.py:18
  208.3 4.1 copy.20
  216.6 18.5 %bitcast_subtract_fusion = f32[3840,512]{0,1:T(8,128)S(1)} fusion(f32[512,3840]{1,0:T(8,128)} %fusion.1, f32[512,3840]{1,0:T(8,128)} %fusion.3, f32[3840,512]{0,1:T(8,128)} %copy.16, f32[512,3840]{1,0:T(8,128)} %fusion.5, f32[256,512]{0,1:T(8,128)} %copy-done, f32[4096,1024]{1,0:T(8,128)} %param.5), kind=kOutput, calls=%fused_computation.2 | convolution fusion | flops 6047662080 | bytes 43778048 | tf_op jit(solution)/shard_map/dot_general | solution.py:18
  235.0 2.0 pad_maximum_fusion
  237.1 4.2 copy.22
  241.3 5.7 %all-to-all-start = ((f32[4,1024,512]{1,2,0:T(8,128)}), f32[4,1024,512]{1,2,0:T(8,128)}, u32[]{:S(2)}, u32[]{:S(2)}) async-start(f32[4,1024,512]{1,2,0:T(8,128)} %bitcast.92), calls=%async_computation | async-start | bytes 16777216 | tf_op jit(solution)/shard_map/all_to_all | solution.py:54
  247.0 32.9 %all-gather.10.cloned.1.call-done = f32[2048,2048]{1,0:T(8,128)} async-done(((f32[256,2048]{1,0:T(8,128)}), f32[2048,2048]{1,0:T(8,128)}) %all-gather.10.cloned.1.call-update) | async-done | bytes 16777232 | tf_op jit(solution)/shard_map/all_gather | solution.py:55
  279.9 151.3 %all-to-all-done = f32[4,1024,512]{1,2,0:T(8,128)} async-done(((f32[4,1024,512]{1,2,0:T(8,128)}), f32[4,1024,512]{1,2,0:T(8,128)}, u32[]{:S(2)}, u32[]{:S(2)}) %all-to-all-start) | async-done | bytes 8388640 | tf_op jit(solution)/shard_map/all_to_all | solution.py:54
  431.2 110.1 %fusion.31 = f32[1024,2048]{1,0:T(8,128)} fusion(f32[1024,2048]{0,1:T(8,128)} %bitcast.17, f32[2048,2048]{1,0:T(8,128)} %all-gather.10.cloned.1.call-done), kind=kOutput, calls=%fused_computation.48 | convolution fusion | flops 51539607552 | bytes 33554432 | tf_op jit(solution)/shard_map/dot_general | solution.py:22
  (23 shorter events, 11.2 us)
Async XLA Ops:
  6.5 42.0 %all-gather.12.cloned.1.call-start = ((), (), s32[]{:S(2)}) async-start(), calls=%async_computation.2 | async-start | bytes 4718592 | tf_op jit(solution)/shard_map/all_gather | solution.py:8
  9.1 84.2 %all-gather.14.cloned.1.call-start = ((), (), s32[]{:S(2)}) async-start(), calls=%async_computation.3 | async-start | bytes 4718592 | tf_op jit(solution)/shard_map/all_gather | solution.py:8
  55.8 85.0 %all-gather.16.cloned.1.call-start = ((), (), s32[]{:S(2)}) async-start(), calls=%async_computation.4 | async-start | bytes 4718592 | tf_op jit(solution)/shard_map/all_gather | solution.py:8
  103.4 104.9 %all-gather.18.cloned.1.call-start = ((), (), s32[]{:S(2)}) async-start(), calls=%async_computation.5 | async-start | bytes 4718592 | tf_op jit(solution)/shard_map/all_gather | solution.py:8
  150.9 129.0 %all-gather.10.cloned.1.call-start = ((), (), s32[]{:S(2)}) async-start(), calls=%async_computation.1 | async-start | bytes 18874368 | tf_op jit(solution)/shard_map/all_gather | solution.py:55
  213.7 1.9 copy-start
  241.3 189.9 %all-to-all-start = ((f32[4,1024,512]{1,2,0:T(8,128)}), f32[4,1024,512]{1,2,0:T(8,128)}, u32[]{:S(2)}, u32[]{:S(2)}) async-start(f32[4,1024,512]{1,2,0:T(8,128)} %bitcast.92), calls=%async_computation | async-start | bytes 16777216 | tf_op jit(solution)/shard_map/all_to_all | solution.py:54
Sparse Core Ops, SparseCore 0:
  9.2 39.2 all-gather.11
  56.0 37.3 all-gather.13
  103.5 37.3 all-gather.15
  151.0 37.3 all-gather.17
  190.1 89.7 all-gather.9
